TPU v7x, 32 devices: a whole 2x2x4 slice. The times are simulated.
32 devices in a mesh: rows: 32 (over z, y, x, core).
Axes of the slice: x: 2, y: 2, z: 4, core: 2. Of those that a mesh axis runs over, the one named last changes fastest.
Arguments:
- snapshots: float32 [262144, 128], P('rows')
- send_list: int32 [1024, 64], P('rows'), may hold values from 0 to 8191
- stencil: int32 [524288, 8], P('rows'), may hold values from 0 to 2047, as said below
- weights: float32 [524288, 8], P('rows'), may hold values from 0.2 to 1
Outputs:
- basis: float32 [524288, 128], P('rows')
- r_factor: float32 [128, 128], replicated
Inputs may be any that keep to these rules, and one draw needn't show every extreme that they name: `send_list`: every slot carries a node; a node may fill several slots. `stencil`: all 8 donors of a row lie on one peer: local row k of device d takes them from peer (d + k // 512) mod 32. Every slot that a device receives is read by some of its rows.
All inputs are finite; a program needn't handle non-finite values.
Results may differ from a plain program's by a relative error of at most 0.0003.
Values sent between devices are 32-bit elements; how exact they have to be, the bound alone decides.
No kernel may reach another device: no remote copies, remote signals or barrier semaphores. Data moves between devices by JAX's collectives and lax.ppermute only.
A program may use at most 192 MiB of HBM per device.

v0:
```python
import jax
import jax.numpy as jnp
from jax import lax
from jax.sharding import PartitionSpec as P


def product(left, right):
    return jnp.dot(left, right, precision=lax.Precision.HIGHEST, preferred_element_type=jnp.float32)


def upper_inverse(upper):
    count = upper.shape[0]
    if count == 1:
        return 1.0 / upper
    half = count // 2
    top_inv = upper_inverse(upper[:half, :half])
    low_inv = upper_inverse(upper[half:, half:])
    corner = -product(product(top_inv, upper[:half, half:]), low_inv)
    zeros_block = jnp.zeros((count - half, half), jnp.float32)
    top_rows = jnp.concatenate([top_inv, corner], axis=1)
    low_rows = jnp.concatenate([zeros_block, low_inv], axis=1)
    return jnp.concatenate([top_rows, low_rows], axis=0)


def normed_factor(block, total_rows):
    local = product(block.T, block)
    gram = lax.psum(local, "rows")
    upper = jnp.linalg.cholesky(gram / total_rows).T
    return upper


def body(snapshots, send_list, stencil, weights):
    peers = lax.axis_size("rows")
    row_count = stencil.shape[0]
    total_rows = row_count * peers
    outgoing = snapshots[send_list]
    received = lax.all_to_all(outgoing, "rows", split_axis=0, concat_axis=0, tiled=True)
    flat = received.reshape(received.shape[0] * received.shape[1], received.shape[2])
    field = jnp.zeros((row_count, flat.shape[1]), jnp.float32)
    for s in range(stencil.shape[1]):
        field = field + weights[:, s][:, None] * flat[stencil[:, s]]
    first = normed_factor(field, total_rows)
    middle = product(field, upper_inverse(first))
    second = normed_factor(middle, total_rows)
    basis = product(middle, upper_inverse(second))
    r_factor = product(second, first)
    return (basis, r_factor)


def solution(mesh):
    return jax.shard_map(
        body,
        mesh=mesh,
        in_specs=(P("rows", None), P("rows", None), P("rows", None), P("rows", None)),
        out_specs=(P("rows", None), P()),
        check_vma=False,
    )
```

profile of v0, /device:TPU:1, one launch (start us, length us, event | category | flops | bytes accessed | tf_op | source)
XLA Modules:
  0.0 1185.2 jit_solution(2221506955138115921)
XLA Ops:
  8.1 9.8 gather_fusion
  17.9 7.1 all-to-all-start
  25.9 1.1 fusion.1773
  27.0 23.3 %all-to-all-done = f32[32,64,128]{2,1,0:T(8,128)S(1)} async-done(((f32[32,64,128]{2,1,0:T(8,128)}), f32[32,64,128]{2,1,0:T(8,128)S(1)}, u32[]{:S(2)}, u32[]{:S(2)}) %all-to-all-start) | async-done | bytes 1048608 | tf_op jit(solution)/shard_map/all_to_all | solution.py:37
  50.3 54.7 %gather_fusion.1 = f32[16384,128]{1,0:T(8,128)} fusion(f32[2048,128]{1,0:T(8,128)S(1)} %bitcast.288, s32[16384]{0:T(1024)S(1)} %broadcast_clamp_fusion.7), kind=kCustom, calls=%fused_computation.1 | custom fusion | bytes 16842752 | tf_op jit(solution)/shard_map/gather | solution.py:41
  105.1 54.8 %gather_fusion.2 = f32[16384,128]{1,0:T(8,128)} fusion(f32[2048,128]{1,0:T(8,128)S(1)} %bitcast.289, s32[16384]{0:T(1024)S(1)} %broadcast_clamp_fusion.6), kind=kCustom, calls=%fused_computation.2 | custom fusion | bytes 16842752 | tf_op jit(solution)/shard_map/gather | solution.py:41
  159.9 54.8 %gather_fusion.3 = f32[16384,128]{1,0:T(8,128)} fusion(f32[2048,128]{1,0:T(8,128)S(1)} %bitcast.290, s32[16384]{0:T(1024)S(1)} %broadcast_clamp_fusion.5), kind=kCustom, calls=%fused_computation.3 | custom fusion | bytes 16842752 | tf_op jit(solution)/shard_map/gather | solution.py:41
  214.6 54.8 %gather_fusion.4 = f32[16384,128]{1,0:T(8,128)} fusion(f32[2048,128]{1,0:T(8,128)S(1)} %bitcast.291, s32[16384]{0:T(1024)S(1)} %broadcast_clamp_fusion.4), kind=kCustom, calls=%fused_computation.4 | custom fusion | bytes 16842752 | tf_op jit(solution)/shard_map/gather | solution.py:41
  269.4 54.8 %gather_fusion.5 = f32[16384,128]{1,0:T(8,128)} fusion(f32[2048,128]{1,0:T(8,128)S(1)} %bitcast.292, s32[16384]{0:T(1024)S(1)} %broadcast_clamp_fusion.3), kind=kCustom, calls=%fused_computation.5 | custom fusion | bytes 16842752 | tf_op jit(solution)/shard_map/gather | solution.py:41
  324.2 54.8 %gather_fusion.6 = f32[16384,128]{1,0:T(8,128)} fusion(f32[2048,128]{1,0:T(8,128)S(1)} %bitcast.293, s32[16384]{0:T(1024)S(1)} %broadcast_clamp_fusion.2), kind=kCustom, calls=%fused_computation.6 | custom fusion | bytes 16842752 | tf_op jit(solution)/shard_map/gather | solution.py:41
  379.0 54.7 %gather_fusion.7 = f32[16384,128]{1,0:T(8,128)} fusion(f32[2048,128]{1,0:T(8,128)S(1)} %bitcast.294, s32[16384]{0:T(1024)S(1)} %broadcast_clamp_fusion.1), kind=kCustom, calls=%fused_computation.7 | custom fusion | bytes 16842752 | tf_op jit(solution)/shard_map/gather | solution.py:41
  433.8 54.9 %gather_fusion.8 = f32[16384,128]{1,0:T(8,128)} fusion(f32[2048,128]{1,0:T(8,128)S(1)} %bitcast.295, s32[16384]{0:T(1024)S(1)} %broadcast_clamp_fusion), kind=kCustom, calls=%fused_computation.8 | custom fusion | bytes 16842752 | tf_op jit(solution)/shard_map/gather | solution.py:41
  488.7 25.8 %multiply_add_fusion = f32[16384,128]{1,0:T(8,128)S(1)} fusion(f32[16384,128]{1,0:T(8,128)} %gather_fusion.8, f32[16384,128]{1,0:T(8,128)} %gather_fusion.7, f32[16384,128]{1,0:T(8,128)} %gather_fusion.6, f32[16384,128]{1,0:T(8,128)} %gather_fusion.5, f32[16384,128]{1,0:T(8,128)} %gather_fusion.4, f32[16384,128]{1,0:T(8,128)} %gather_fusion.3, ...), kind=kLoop, calls=%fused_computation.9 | loop fusion | flops 31457280 | bytes 76021760 | tf_op jit(solution)/shard_map/add | solution.py:41
  514.5 3.4 copy-done.1
  517.9 14.9 %fusion.1794 = f32[128,128]{0,1:T(8,128)} fusion(f32[16384,128]{1,0:T(8,128)S(1)} %multiply_add_fusion), kind=kOutput, calls=%fused_computation.2092 | convolution fusion | flops 3221225472 | bytes 8454144 | tf_op jit(solution)/shard_map/dot_general | solution.py:8
  532.8 118.9 %all-reduce.129.cloned.1.call-done = f32[128,128]{0,1:T(8,128)} async-done(((f32[128,128]{0,1:T(8,128)}), f32[128,128]{0,1:T(8,128)}) %all-reduce.129.cloned.1.call-update) | async-done | bytes 65552 | tf_op jit(solution)/shard_map/psum | solution.py:27
  653.5 11.7 cholesky.44
  831.1 10.1 fusion.13
  841.2 3.3 copy-done
  844.5 14.6 %fusion.1795 = f32[128,128]{0,1:T(8,128)} fusion(f32[16384,128]{1,0:T(8,128)S(1)} %fusion.13), kind=kOutput, calls=%fused_computation.2093 | convolution fusion | flops 3221225472 | bytes 8454144 | tf_op jit(solution)/shard_map/dot_general | solution.py:8
  859.1 118.5 %all-reduce.131.cloned.1.call-done = f32[128,128]{0,1:T(8,128)} async-done(((f32[128,128]{0,1:T(8,128)}), f32[128,128]{0,1:T(8,128)}) %all-reduce.131.cloned.1.call-update) | async-done | bytes 65552 | tf_op jit(solution)/shard_map/psum | solution.py:27
  979.4 11.7 cholesky.55
  991.8 2.1 fusion.66
  1160.7 17.2 %fusion.28 = f32[16384,128]{1,0:T(8,128)} fusion(f32[16384,128]{1,0:T(8,128)} %copy-done, f32[1,1]{0,1:T(1,128)} %constant.46.clone.1, f32[64,64]{0,1:T(8,128)S(1)} %fusion.116, f32[64,64]{0,1:T(8,128)S(1)} %convolution_negate_fusion, f32[32,64]{0,1:T(8,128)S(1)} %concatenate.2854, f32[32,32]{0,1:T(8,128)S(1)} %convolution_negate_fusion.3, ...), kind=kOutput, calls=%fused_computation.185 | convolution fusion | flops 3221504000 | bytes 16826368 | tf_op jit(solution)/shard_map/dot_general | solution.py:8
  (502 shorter events, 86.9 us)
Async XLA Ops:
  7.2 17.9 %copy-start.2 = (s32[16384,8]{0,1:T(8,128)S(1)}, s32[16384,8]{0,1:T(8,128)}, u32[]{:S(2)}) copy-start(s32[16384,8]{0,1:T(8,128)} %param.7) | copy-start | bytes 1572868
  7.2 18.7 %copy-start.3 = (f32[16384,8]{0,1:T(8,128)S(1)}, f32[16384,8]{0,1:T(8,128)}, u32[]{:S(2)}) copy-start(f32[16384,8]{0,1:T(8,128)} %param.8) | copy-start | bytes 1572868
  17.9 32.4 %all-to-all-start = ((f32[32,64,128]{2,1,0:T(8,128)}), f32[32,64,128]{2,1,0:T(8,128)S(1)}, u32[]{:S(2)}, u32[]{:S(2)}) async-start(f32[32,64,128]{2,1,0:T(8,128)} %bitcast.1), calls=%async_computation | async-start | bytes 2097152 | tf_op jit(solution)/shard_map/all_to_all | solution.py:37
  25.0 626.7 %all-reduce.129.cloned.1.call-start = ((), (), s32[]{:S(2)}) async-start(), calls=%async_computation.1 | async-start | bytes 131072 | tf_op jit(solution)/shard_map/psum | solution.py:27
  433.7 54.9 %copy-start.4 = (f32[16384,1]{0,1:T(1,128)S(1)}, f32[16384,1]{0,1:T(1,128)}, u32[]{:S(2)}) copy-start(f32[16384,1]{0,1:T(1,128)} %get-tuple-element.3) | copy-start | bytes 196612
  433.7 54.9 %copy-start.5 = (f32[16384,1]{0,1:T(1,128)S(1)}, f32[16384,1]{0,1:T(1,128)}, u32[]{:S(2)}) copy-start(f32[16384,1]{0,1:T(1,128)} %get-tuple-element.4) | copy-start | bytes 196612
  433.7 54.9 %copy-start.6 = (f32[16384,1]{0,1:T(1,128)S(1)}, f32[16384,1]{0,1:T(1,128)}, u32[]{:S(2)}) copy-start(f32[16384,1]{0,1:T(1,128)} %get-tuple-element.5) | copy-start | bytes 196612
  433.7 54.9 %copy-start.7 = (f32[16384,1]{0,1:T(1,128)S(1)}, f32[16384,1]{0,1:T(1,128)}, u32[]{:S(2)}) copy-start(f32[16384,1]{0,1:T(1,128)} %get-tuple-element.6) | copy-start | bytes 196612
  433.8 54.9 %copy-start.8 = (f32[16384,1]{0,1:T(1,128)S(1)}, f32[16384,1]{0,1:T(1,128)}, u32[]{:S(2)}) copy-start(f32[16384,1]{0,1:T(1,128)} %get-tuple-element.7) | copy-start | bytes 196612
  433.8 54.9 %copy-start.9 = (f32[16384,1]{0,1:T(1,128)S(1)}, f32[16384,1]{0,1:T(1,128)}, u32[]{:S(2)}) copy-start(f32[16384,1]{0,1:T(1,128)} %get-tuple-element.8) | copy-start | bytes 196612
  433.8 54.9 %copy-start.10 = (f32[16384,1]{0,1:T(1,128)S(1)}, f32[16384,1]{0,1:T(1,128)}, u32[]{:S(2)}) copy-start(f32[16384,1]{0,1:T(1,128)} %get-tuple-element.9) | copy-start | bytes 196612
  433.8 54.9 %copy-start.11 = (f32[16384,1]{0,1:T(1,128)S(1)}, f32[16384,1]{0,1:T(1,128)}, u32[]{:S(2)}) copy-start(f32[16384,1]{0,1:T(1,128)} %get-tuple-element.10) | copy-start | bytes 196612
  514.5 3.4 copy-start.1
  532.8 444.8 %all-reduce.131.cloned.1.call-start = ((), (), s32[]{:S(2)}) async-start(), calls=%async_computation.2 | async-start | bytes 131072 | tf_op jit(solution)/shard_map/psum | solution.py:27
  841.2 3.3 copy-start
Sparse Core Ops, SparseCore 0:
  532.9 118.7 all-reduce.128
  859.2 118.3 all-reduce.130
where the time goes:
time: 1190 us
  local copies, waits for them, and re-layouts  474 us (40%)
  between operations  267 us (22%)
  waiting for transfers between devices  261 us (22%)
  matrix products  111 us (9%)
  other arithmetic  66.1 us (6%)
    gather x8, local copies, waits for them, and re-layouts, body(): field = field + weights[:, s][:, None] * flat[stencil[:, s]]  438 us
    psum x2, waiting for transfers between devices, normed_factor(): gram = lax.psum(local, 'rows')  237 us
    dot_general x257, matrix products, product(): jnp.dot(left, right, precision=lax.Precision.HIGHEST, preferred_element_t...  111 us
    add x1, other arithmetic, body(): field = field + weights[:, s][:, None] * flat[stencil[:, s]]  25.8 us
    another operation x6, other arithmetic, normed_factor(): upper = jnp.linalg.cholesky(gram / total_rows).T  24.8 us
  transfers between devices with their start and end apart: 3, of which 3 were waited for; matrix products, arithmetic and copies ran while one was open for 0% of the time, Pallas kernels for 0%

commit v1 on v0

--- a/solution.py
+++ b/solution.py
@@ -24,7 +24,10 @@
 
 def normed_factor(block, total_rows):
     local = product(block.T, block)
-    gram = lax.psum(local, "rows")
+    devices, gram = (lax.axis_size("rows"), local)
+    for hop in [1 << k for k in range(devices.bit_length() - 1)]:
+        pairs = [(i, i ^ hop) for i in range(devices)]
+        gram = gram + lax.ppermute(gram, "rows", pairs)
     upper = jnp.linalg.cholesky(gram / total_rows).T
     return upper
 

time: 1190 us -> 972 us (0.82)
  waiting for transfers between devices: 261 us -> 46.3 us
  between operations: 267 us -> 253 us
  starting transfers between devices: 7.18 us -> 20.9 us
    psum x2 -> x0, waiting for transfers between devices: 237 us -> none  [normed_factor(): gram = lax.psum(local, 'rows')]
    ppermute x0 -> x10, waiting for transfers between devices: none -> 22.9 us  [normed_factor(): gram = gram + lax.ppermute(gram, 'rows', pairs)]
    ppermute x0 -> x10, starting transfers between devices: none -> 13.8 us  [normed_factor(): gram = gram + lax.ppermute(gram, 'rows', pairs)]
  transfers between devices with their start and end apart: 3 -> 11, of which waited for: 3 -> 11; matrix products, arithmetic and copies ran while one was open for 0% -> 0% of each run, Pallas kernels for 0% -> 0%
where the time goes in v1:
time: 972 us; the launch traced here: 960 us
  local copies, waits for them, and re-layouts  467 us (48%)
  between operations  253 us (26%)
  matrix products  110 us (11%)
  other arithmetic  63.1 us (6%)
  waiting for transfers between devices  46.3 us (5%)
  starting transfers between devices  20.9 us (2%)
    gather x8, local copies, waits for them, and re-layouts, body(): field = field + weights[:, s][:, None] * flat[stencil[:, s]]  438 us
    dot_general x257, matrix products, product(): jnp.dot(left, right, precision=lax.Precision.HIGHEST, preferred_element_t...  110 us
    add x1, other arithmetic, body(): field = field + weights[:, s][:, None] * flat[stencil[:, s]]  25.9 us
    another operation x6, other arithmetic, normed_factor(): upper = jnp.linalg.cholesky(gram / total_rows).T  24.8 us
    all_to_all x1, waiting for transfers between devices, body(): lax.all_to_all(outgoing, 'rows', split_axis=0, concat_axis=0, tiled=True)  23.4 us
    ppermute x10, waiting for transfers between devices, normed_factor(): gram = gram + lax.ppermute(gram, 'rows', pairs)  22.9 us
  transfers between devices with their start and end apart: 11, of which 11 were waited for; matrix products, arithmetic and copies ran while one was open for 0% of the time, Pallas kernels for 0%

profile of v1, /device:TPU:1, one launch (start us, length us, event | category | flops | bytes accessed | tf_op | source)
XLA Modules:
  0.0 960.2 jit_solution(1155112433441242662)
XLA Ops:
  1.5 9.8 %gather_fusion = f32[2048,128]{1,0:T(8,128)} fusion(f32[8192,128]{1,0:T(8,128)} %param.5, s32[2048]{0:T(1024)S(1)} %broadcast_clamp_fusion.8), kind=kCustom, calls=%fused_computation | custom fusion | bytes 2105344 | tf_op jit(solution)/shard_map/gather | solution.py:39
  11.4 7.1 all-to-all-start
  20.4 23.4 %all-to-all-done = f32[32,64,128]{2,1,0:T(8,128)S(1)} async-done(((f32[32,64,128]{2,1,0:T(8,128)}), f32[32,64,128]{2,1,0:T(8,128)S(1)}, u32[]{:S(2)}, u32[]{:S(2)}) %all-to-all-start) | async-done | bytes 1048608 | tf_op jit(solution)/shard_map/all_to_all | solution.py:40
  43.8 54.8 %gather_fusion.1 = f32[16384,128]{1,0:T(8,128)} fusion(f32[2048,128]{1,0:T(8,128)S(1)} %bitcast.288, s32[16384]{0:T(1024)S(1)} %broadcast_clamp_fusion.7), kind=kCustom, calls=%fused_computation.1 | custom fusion | bytes 16842752 | tf_op jit(solution)/shard_map/gather | solution.py:44
  98.6 54.8 %gather_fusion.2 = f32[16384,128]{1,0:T(8,128)} fusion(f32[2048,128]{1,0:T(8,128)S(1)} %bitcast.289, s32[16384]{0:T(1024)S(1)} %broadcast_clamp_fusion.6), kind=kCustom, calls=%fused_computation.2 | custom fusion | bytes 16842752 | tf_op jit(solution)/shard_map/gather | solution.py:44
  153.3 54.8 %gather_fusion.3 = f32[16384,128]{1,0:T(8,128)} fusion(f32[2048,128]{1,0:T(8,128)S(1)} %bitcast.290, s32[16384]{0:T(1024)S(1)} %broadcast_clamp_fusion.5), kind=kCustom, calls=%fused_computation.3 | custom fusion | bytes 16842752 | tf_op jit(solution)/shard_map/gather | solution.py:44
  208.1 54.8 %gather_fusion.4 = f32[16384,128]{1,0:T(8,128)} fusion(f32[2048,128]{1,0:T(8,128)S(1)} %bitcast.291, s32[16384]{0:T(1024)S(1)} %broadcast_clamp_fusion.4), kind=kCustom, calls=%fused_computation.4 | custom fusion | bytes 16842752 | tf_op jit(solution)/shard_map/gather | solution.py:44
  262.9 54.7 %gather_fusion.5 = f32[16384,128]{1,0:T(8,128)} fusion(f32[2048,128]{1,0:T(8,128)S(1)} %bitcast.292, s32[16384]{0:T(1024)S(1)} %broadcast_clamp_fusion.3), kind=kCustom, calls=%fused_computation.5 | custom fusion | bytes 16842752 | tf_op jit(solution)/shard_map/gather | solution.py:44
  317.6 54.9 %gather_fusion.6 = f32[16384,128]{1,0:T(8,128)} fusion(f32[2048,128]{1,0:T(8,128)S(1)} %bitcast.293, s32[16384]{0:T(1024)S(1)} %broadcast_clamp_fusion.2), kind=kCustom, calls=%fused_computation.6 | custom fusion | bytes 16842752 | tf_op jit(solution)/shard_map/gather | solution.py:44
  372.5 54.8 %gather_fusion.7 = f32[16384,128]{1,0:T(8,128)} fusion(f32[2048,128]{1,0:T(8,128)S(1)} %bitcast.294, s32[16384]{0:T(1024)S(1)} %broadcast_clamp_fusion.1), kind=kCustom, calls=%fused_computation.7 | custom fusion | bytes 16842752 | tf_op jit(solution)/shard_map/gather | solution.py:44
  427.3 54.9 %gather_fusion.8 = f32[16384,128]{1,0:T(8,128)} fusion(f32[2048,128]{1,0:T(8,128)S(1)} %bitcast.295, s32[16384]{0:T(1024)S(1)} %broadcast_clamp_fusion), kind=kCustom, calls=%fused_computation.8 | custom fusion | bytes 16842752 | tf_op jit(solution)/shard_map/gather | solution.py:44
  482.2 25.9 %multiply_add_fusion = f32[16384,128]{1,0:T(8,128)S(1)} fusion(f32[16384,128]{1,0:T(8,128)} %gather_fusion.8, f32[16384,128]{1,0:T(8,128)} %gather_fusion.7, f32[16384,128]{1,0:T(8,128)} %gather_fusion.6, f32[16384,128]{1,0:T(8,128)} %gather_fusion.5, f32[16384,128]{1,0:T(8,128)} %gather_fusion.4, f32[16384,128]{1,0:T(8,128)} %gather_fusion.3, ...), kind=kLoop, calls=%fused_computation.9 | loop fusion | flops 31457280 | bytes 76021760 | tf_op jit(solution)/shard_map/add | solution.py:44
  508.1 14.4 %fusion.1794 = f32[128,128]{0,1:T(8,128)S(1)} fusion(f32[16384,128]{1,0:T(8,128)S(1)} %multiply_add_fusion), kind=kOutput, calls=%fused_computation.2092 | convolution fusion | flops 3221225472 | bytes 8454144 | tf_op jit(solution)/shard_map/dot_general | solution.py:8
  531.6 2.6 collective-permute-done.3
  535.8 3.2 collective-permute-done.4
  539.1 11.7 %cholesky.44 = f32[128,128]{1,0:T(8,128)S(1)} custom-call(f32[128,128]{1,0:T(8,128)S(1)} %fusion.65), custom_call_target="Cholesky" | custom-call | tf_op jit(solution)/shard_map/jit(cholesky)/cholesky | solution.py:31
  716.7 9.9 %fusion.13 = f32[16384,128]{1,0:T(8,128)S(1)} fusion(f32[16384,128]{1,0:T(8,128)} %copy-done.1, f32[1,1]{0,1:T(1,128)} %constant.46.clone.1, f32[64,64]{0,1:T(8,128)S(1)} %fusion.92, f32[64,64]{0,1:T(8,128)S(1)} %convolution_negate_fusion.1, f32[32,64]{0,1:T(8,128)S(1)} %concatenate.2473, f32[32,32]{0,1:T(8,128)S(1)} %convolution_negate_fusion.5, ...), kind=kOutput, calls=%fused_computation.171 | convolution fusion | flops 3221504000 | bytes 16826368 | tf_op jit(solution)/shard_map/dot_general | solution.py:8
  726.6 14.2 %fusion.1795 = f32[128,128]{0,1:T(8,128)S(1)} fusion(f32[16384,128]{1,0:T(8,128)S(1)} %fusion.13), kind=kOutput, calls=%fused_computation.2093 | convolution fusion | flops 3221225472 | bytes 8454144 | tf_op jit(solution)/shard_map/dot_general | solution.py:8
  740.8 5.0 collective-permute-start.5
  747.3 2.6 collective-permute-done.6
  753.6 2.7 collective-permute-done.8
  756.9 4.2 collective-permute-done.9
  761.2 11.7 %cholesky.55 = f32[128,128]{1,0:T(8,128)S(1)} custom-call(f32[128,128]{1,0:T(8,128)S(1)} %fusion.64), custom_call_target="Cholesky" | custom-call | tf_op jit(solution)/shard_map/jit(cholesky)/cholesky | solution.py:31
  942.8 17.2 %fusion.28 = f32[16384,128]{1,0:T(8,128)} fusion(f32[16384,128]{1,0:T(8,128)} %copy-done, f32[1,1]{0,1:T(1,128)} %constant.46.clone.1, f32[64,64]{0,1:T(8,128)S(1)} %fusion.116, f32[64,64]{0,1:T(8,128)S(1)} %convolution_negate_fusion, f32[32,64]{0,1:T(8,128)S(1)} %concatenate.2854, f32[32,32]{0,1:T(8,128)S(1)} %convolution_negate_fusion.3, ...), kind=kOutput, calls=%fused_computation.185 | convolution fusion | flops 3221504000 | bytes 16826368 | tf_op jit(solution)/shard_map/dot_general | solution.py:8
  (524 shorter events, 103.2 us)
Async XLA Ops:
  0.6 17.8 %copy-start.2 = (s32[16384,8]{0,1:T(8,128)S(1)}, s32[16384,8]{0,1:T(8,128)}, u32[]{:S(2)}) copy-start(s32[16384,8]{0,1:T(8,128)} %param.7) | copy-start | bytes 1572868
  0.6 18.7 %copy-start.3 = (f32[16384,8]{0,1:T(8,128)S(1)}, f32[16384,8]{0,1:T(8,128)}, u32[]{:S(2)}) copy-start(f32[16384,8]{0,1:T(8,128)} %param.8) | copy-start | bytes 1572868
  11.4 32.4 %all-to-all-start = ((f32[32,64,128]{2,1,0:T(8,128)}), f32[32,64,128]{2,1,0:T(8,128)S(1)}, u32[]{:S(2)}, u32[]{:S(2)}) async-start(f32[32,64,128]{2,1,0:T(8,128)} %bitcast.1), calls=%async_computation | async-start | bytes 2097152 | tf_op jit(solution)/shard_map/all_to_all | solution.py:40
  427.3 54.9 %copy-start.4 = (f32[16384,1]{0,1:T(1,128)S(1)}, f32[16384,1]{0,1:T(1,128)}, u32[]{:S(2)}) copy-start(f32[16384,1]{0,1:T(1,128)} %get-tuple-element.3) | copy-start | bytes 196612
  427.3 54.9 %copy-start.5 = (f32[16384,1]{0,1:T(1,128)S(1)}, f32[16384,1]{0,1:T(1,128)}, u32[]{:S(2)}) copy-start(f32[16384,1]{0,1:T(1,128)} %get-tuple-element.4) | copy-start | bytes 196612
  427.3 54.9 %copy-start.6 = (f32[16384,1]{0,1:T(1,128)S(1)}, f32[16384,1]{0,1:T(1,128)}, u32[]{:S(2)}) copy-start(f32[16384,1]{0,1:T(1,128)} %get-tuple-element.5) | copy-start | bytes 196612
  427.3 54.9 %copy-start.7 = (f32[16384,1]{0,1:T(1,128)S(1)}, f32[16384,1]{0,1:T(1,128)}, u32[]{:S(2)}) copy-start(f32[16384,1]{0,1:T(1,128)} %get-tuple-element.6) | copy-start | bytes 196612
  427.3 54.9 %copy-start.8 = (f32[16384,1]{0,1:T(1,128)S(1)}, f32[16384,1]{0,1:T(1,128)}, u32[]{:S(2)}) copy-start(f32[16384,1]{0,1:T(1,128)} %get-tuple-element.7) | copy-start | bytes 196612
  427.3 54.9 %copy-start.9 = (f32[16384,1]{0,1:T(1,128)S(1)}, f32[16384,1]{0,1:T(1,128)}, u32[]{:S(2)}) copy-start(f32[16384,1]{0,1:T(1,128)} %get-tuple-element.8) | copy-start | bytes 196612
  427.3 54.9 %copy-start.10 = (f32[16384,1]{0,1:T(1,128)S(1)}, f32[16384,1]{0,1:T(1,128)}, u32[]{:S(2)}) copy-start(f32[16384,1]{0,1:T(1,128)} %get-tuple-element.9) | copy-start | bytes 196612
  427.3 54.9 %copy-start.11 = (f32[16384,1]{0,1:T(1,128)S(1)}, f32[16384,1]{0,1:T(1,128)}, u32[]{:S(2)}) copy-start(f32[16384,1]{0,1:T(1,128)} %get-tuple-element.10) | copy-start | bytes 196612
  508.1 14.4 %copy-start.1 = (f32[16384,128]{1,0:T(8,128)}, f32[16384,128]{1,0:T(8,128)S(1)}, u32[]{:S(2)}) copy-start(f32[16384,128]{1,0:T(8,128)S(1)} %multiply_add_fusion) | copy-start | bytes 25165828
  522.5 2.1 collective-permute-start
  524.6 3.2 collective-permute-start.1
  527.8 3.2 collective-permute-start.2
  531.0 3.2 collective-permute-start.3
  534.2 4.8 collective-permute-start.4
  726.6 14.2 %copy-start = (f32[16384,128]{1,0:T(8,128)}, f32[16384,128]{1,0:T(8,128)S(1)}, u32[]{:S(2)}) copy-start(f32[16384,128]{1,0:T(8,128)S(1)} %fusion.13) | copy-start | bytes 25165828
  740.8 5.9 collective-permute-start.5
  746.7 3.2 collective-permute-start.6
  749.9 3.2 collective-permute-start.7
  753.1 3.2 collective-permute-start.8
  756.3 4.8 collective-permute-start.9
